TPU v7x, 32 devices: a whole 2x2x4 slice. The times are simulated.
32 devices in a mesh: layer: 2 (over x), expert: 4 (over y, core), col: 4 (over z).
Axes of the slice: x: 2, y: 2, z: 4, core: 2. Of those that a mesh axis runs over, the one named last changes fastest.
Arguments:
- target_weights: bfloat16 [8, 7168, 2048], P(('layer', 'expert'), None, 'col'), parts along dimension 0, may hold values from -36 to 36
- factors: float32 [8, 7168, 128], P(('layer', 'expert'), 'col'), parts along dimension 0, may hold values from -0.5 to 0.5
- bases: float32 [64, 128, 2048], P('layer', None, 'col'), parts along dimension 0, may hold values from -6 to 6
- coefficients: float32 [8, 32], P(('layer', 'expert')), parts along dimension 0, may hold values from -1 to 1
Outputs:
- new_factors: float32 [8, 7168, 128], P(('layer', 'expert'), 'col'), parts along dimension 0
- new_bases: float32 [64, 128, 2048], P('layer', None, 'col'), parts along dimension 0
- new_coefficients: float32 [8, 32], P(('layer', 'expert')), parts along dimension 0
- losses: float32 [4], P('layer'), parts along dimension 0
There are 2 independent parts, one for each index of `layer`. A program takes and returns all parts, laid end to end along the dimension named above; each array names one. Nothing has to cross between parts.
All inputs are finite; a program needn't handle non-finite values.
Results may differ from a plain program's by a relative error of at most 0.0003.
Values sent between devices are 32-bit elements; how exact they have to be, the bound alone decides.
A program may use at most 128 MiB of HBM per device.

v0:
```python
import jax
import jax.numpy as jnp
from jax import lax
from jax.sharding import PartitionSpec as P

D = 7168
H = 2048
ITERS = 2


LEARN_RATE = 0.01
BETA_ONE = 0.9
BETA_TWO = 0.999
EPSILON = 0.0001
HIGHEST = lax.Precision.HIGHEST


def adam_update(parameter, gradient, moment_one, moment_two, iteration):
    moment_one = BETA_ONE * moment_one + (1.0 - BETA_ONE) * gradient
    moment_two = BETA_TWO * moment_two + (1.0 - BETA_TWO) * gradient * gradient
    first_hat = moment_one / (1.0 - BETA_ONE ** (iteration + 1))
    second_hat = moment_two / (1.0 - BETA_TWO ** (iteration + 1))
    parameter = parameter - LEARN_RATE * first_hat / (jnp.sqrt(second_hat) + EPSILON)
    return (parameter, moment_one, moment_two)


def shards(target_weights, factors, bases, coefficients):
    expert_count = lax.axis_size("expert")
    local_experts = target_weights.shape[0]
    basis_share = bases.shape[0] // expert_count
    basis_begin = lax.axis_index("expert") * basis_share
    loss_scale = 1.0 / (2.0 * local_experts * expert_count * D * H)
    own_bases = lax.dynamic_slice_in_dim(bases, basis_begin, basis_share, 0)
    basis_one = jnp.zeros_like(own_bases)
    basis_two = jnp.zeros_like(own_bases)
    coef_one = jnp.zeros_like(coefficients)
    coef_two = jnp.zeros_like(coefficients)
    current_bases = bases
    current_factors = factors
    factor_one = jnp.zeros_like(factors)
    factor_two = jnp.zeros_like(factors)
    loss_values = []
    for iteration in range(ITERS):
        gathered = lax.all_gather(current_factors, "col", axis=1, tiled=True)
        mixed = jnp.tanh(jnp.einsum("ek,krh->erh", coefficients, current_bases, precision=HIGHEST))
        residual = jnp.einsum(
            "edr,erh->edh", gathered, mixed, precision=HIGHEST
        ) - target_weights.astype(jnp.float32)
        loss_part = jnp.sum(residual * residual)
        gradient = residual / H
        d_mixed = jnp.einsum("edr,edh->erh", gathered, gradient, precision=HIGHEST)
        d_pre = d_mixed * (1.0 - mixed * mixed)
        coef_slice = coefficients
        d_basis = lax.psum_scatter(
            jnp.einsum("ek,erh->krh", coef_slice, d_pre, precision=HIGHEST),
            "expert",
            scatter_dimension=0,
            tiled=True,
        )
        d_coef = lax.psum(jnp.einsum("krh,erh->ek", current_bases, d_pre, precision=HIGHEST), "col")
        d_share = lax.psum_scatter(
            jnp.einsum("edh,erh->der", gradient, mixed, precision=HIGHEST),
            "col",
            scatter_dimension=0,
            tiled=True,
        )
        d_share = jnp.transpose(d_share, (1, 0, 2))
        current_factors, factor_one, factor_two = adam_update(
            current_factors, d_share, factor_one, factor_two, iteration
        )
        own_bases, basis_one, basis_two = adam_update(
            own_bases, d_basis, basis_one, basis_two, iteration
        )
        coefficients, coef_one, coef_two = adam_update(
            coefficients, d_coef, coef_one, coef_two, iteration
        )
        current_bases = lax.all_gather(own_bases, "expert", axis=0, tiled=True)
        loss_values.append(lax.psum(loss_part, ("expert", "col")))
    loss_totals = jnp.stack(loss_values)
    return (current_factors, current_bases, coefficients, loss_totals * loss_scale)


def solution(mesh):
    return jax.shard_map(
        shards,
        mesh=mesh,
        in_specs=(
            P(("layer", "expert"), None, "col"),
            P(("layer", "expert"), "col", None),
            P("layer", None, "col"),
            P(("layer", "expert"), None),
        ),
        out_specs=(
            P(("layer", "expert"), "col", None),
            P("layer", None, "col"),
            P(("layer", "expert"), None),
            P("layer"),
        ),
        check_vma=False,
    )
```

profile of v0, /device:TPU:0, one launch (start us, length us, event | category | flops | bytes accessed | tf_op | source)
XLA Modules:
  0.0 658.6 jit_solution(1172919864465616903)
XLA Ops:
  7.2 0.0 all-gather.5.cloned.1.call-start
  7.2 0.7 all-gather.5.cloned.1.call-update
  7.9 0.0 reduce-scatter.7.cloned.1.call-start
  7.9 12.3 %fusion.20 = f32[1,128,512]{2,0,1:T(1,128)S(1)} fusion(f32[32,128,512]{2,1,0:T(8,128)} %param.6, f32[1,32]{1,0:T(1,128)} %param.7), kind=kOutput, calls=%fused_computation.20 | convolution fusion | flops 25165824 | bytes 8650880 | tf_op jit(solution)/shard_map/ek,krh->erh/dot_general | solution.py:45
  20.2 0.1 copy.23
  20.4 10.1 %copy.15 = bf16[1,7168,512]{1,2,0:T(8,128)(2,1)} copy(bf16[1,7168,512]{2,1,0:T(8,128)(2,1)} %param.4) | data formatting | bytes 14680064 | tf_op args[0]
  30.4 54.0 %all-gather.5.cloned.1.call-done = f32[1,7168,128]{2,1,0:T(8,128)} async-done(((f32[1,1792,128]{2,1,0:T(8,128)}), f32[1,7168,128]{2,1,0:T(8,128)}) %all-gather.5.cloned.1.call-update) | async-done | bytes 3670032 | tf_op jit(solution)/shard_map/all_gather | solution.py:44
  84.4 19.3 %multiply_reduce_fusion.1 = (f32[]{:T(128)}, f32[1,7168,512]{1,2,0:T(8,128)S(1)}) fusion(bf16[1,7168,512]{1,2,0:T(8,128)(2,1)} %copy.15, f32[1,7168,128]{2,1,0:T(8,128)} %all-gather.5.cloned.1.call-done, f32[1,128,512]{1,2,0:T(8,128)S(1)} %copy.23), kind=kOutput, calls=%fused_computation.11 | convolution fusion | flops 5651824640 | bytes 25952260 | tf_op jit(solution)/shard_map/edr,erh->edh/dot_general | solution.py:46
  103.7 5.2 copy-done.1
  108.8 0.0 copy-done.4
  108.8 11.8 %fusion.41 = f32[128,512]{0,1:T(8,128)S(1)} fusion(f32[1,7168,128]{2,1,0:T(8,128)S(1)} %copy-done.4, f32[1,7168,512]{1,2,0:T(8,128)S(1)} %get-tuple-element.17, f32[1,128,512]{1,2,0:T(8,128)S(1)} %copy.23), kind=kOutput, calls=%fused_computation.44 | convolution fusion | flops 5641011200 | bytes 18874368 | tf_op jit(solution)/shard_map/edr,edh->erh/dot_general | solution.py:51
  120.6 0.1 copy.17
  120.8 0.0 copy-done.7
  120.8 4.5 multiply_bitcast_fusion
  125.3 0.0 reduce-scatter.7.cloned.1.call-update
  125.3 0.0 reduce-scatter.5.cloned.1.call-start
  125.4 13.9 %fusion.12 = f32[7168,1,128]{0,2,1:T(8,128)} fusion(f32[1,7168,512]{1,2,0:T(8,128)} %copy-done.1, f32[1,128,512]{1,2,0:T(8,128)S(1)} %copy.23), kind=kOutput, calls=%fused_computation.16 | convolution fusion | flops 5640814592 | bytes 18612224 | tf_op jit(solution)/shard_map/edh,erh->der/dot_general | solution.py:62
  139.2 0.0 reduce-scatter.5.cloned.1.call-update
  139.3 0.0 all-gather.7.cloned.1.call-start
  139.3 56.2 %reduce-scatter.7.cloned.1.call-done = f32[8,128,512]{2,1,0:T(8,128)} async-done(((f32[32,128,512]{2,1,0:T(8,128)}), f32[8,128,512]{2,1,0:T(8,128)}) %reduce-scatter.7.cloned.1.call-update) | async-done | bytes 2097168 | tf_op jit(solution)/shard_map/reduce_scatter | solution.py:54
  195.5 4.6 divide_subtract_fusion
  200.1 0.0 all-gather.7.cloned.1.call-update
  200.1 0.0 all-gather.9.cloned.1.call-start
  200.1 0.0 copy-done.5
  200.1 0.3 copy.16
  200.5 65.9 %reduce-scatter.5.cloned.1.call-done = f32[1792,1,128]{0,2,1:T(8,128)} async-done(((f32[7168,1,128]{0,2,1:T(8,128)}), f32[1792,1,128]{0,2,1:T(8,128)}) %reduce-scatter.5.cloned.1.call-update) | async-done | bytes 917520 | tf_op jit(solution)/shard_map/reduce_scatter | solution.py:61
  266.4 2.6 fusion.60
  268.9 0.0 all-gather.9.cloned.1.call-update
  269.0 0.0 reduce-scatter.11.cloned.1.call-start
  269.0 10.5 %copy.25 = f32[32,128,512]{1,0,2:T(8,128)} copy(f32[32,128,512]{2,1,0:T(8,128)} %param.6) | data formatting | bytes 16777216 | tf_op args[2]
  279.5 9.3 %convolution_bitcast_fusion.1 = f32[1,32]{1,0:T(1,128)S(1)} fusion(f32[128,512,1]{0,2,1:T(1,128)S(1)} %bitcast.131, f32[32,128,512]{1,0,2:T(8,128)} %copy.25), kind=kOutput, calls=%fused_computation.47 | convolution fusion | flops 25165824 | bytes 8650880 | tf_op jit(solution)/shard_map/krh,erh->ek/dot_general | solution.py:60
  288.9 11.7 %psum.28 = f32[1,32]{1,0:T(1,128)S(1)} all-reduce(f32[1,32]{1,0:T(1,128)S(1)} %convolution_bitcast_fusion.1), channel_id=1, replica_groups=mesh['layer'=2,'expert'=4,'col'=4] {'col'}, use_global_device_ids=true, to_apply=%region_1.0 | all-reduce | flops 32 | bytes 256 | tf_op jit(solution)/shard_map/psum | solution.py:60
  300.5 25.8 %all-gather.7.cloned.1.call-done = f32[32,128,512]{2,1,0:T(8,128)} async-done(((f32[8,128,512]{2,1,0:T(8,128)}), f32[32,128,512]{2,1,0:T(8,128)}) %all-gather.7.cloned.1.call-update) | async-done | bytes 8388624 | tf_op jit(solution)/shard_map/all_gather | solution.py:77
  326.3 12.3 %fusion.18 = f32[1,128,512]{2,0,1:T(1,128)S(1)} fusion(f32[32,128,512]{2,1,0:T(8,128)} %all-gather.7.cloned.1.call-done, f32[1,32]{1,0:T(1,128)S(1)} %divide_subtract_fusion.2), kind=kOutput, calls=%fused_computation.18 | convolution fusion | flops 25165824 | bytes 8650880 | tf_op jit(solution)/shard_map/ek,krh->erh/dot_general | solution.py:45
  338.6 0.1 copy.27
  338.8 61.7 %all-gather.9.cloned.1.call-done = f32[1,7168,128]{1,2,0:T(8,128)} async-done(((f32[1,1792,128]{1,2,0:T(8,128)}), f32[1,7168,128]{1,2,0:T(8,128)}) %all-gather.9.cloned.1.call-update) | async-done | bytes 3670032 | tf_op jit(solution)/shard_map/all_gather | solution.py:44
  400.4 18.7 %multiply_reduce_fusion = (f32[]{:T(128)}, f32[1,7168,512]{1,2,0:T(8,128)S(1)}) fusion(bf16[1,7168,512]{1,2,0:T(8,128)(2,1)} %copy.15, f32[1,128,512]{1,2,0:T(8,128)S(1)} %copy.27, f32[1,7168,128]{1,2,0:T(8,128)} %all-gather.9.cloned.1.call-done), kind=kOutput, calls=%fused_computation.10 | convolution fusion | flops 5651824640 | bytes 25952260 | tf_op jit(solution)/shard_map/edr,erh->edh/dot_general | solution.py:46
  419.1 5.2 copy-done
  424.3 0.0 copy-done.2
  424.3 11.7 %fusion.46 = f32[128,512]{0,1:T(8,128)S(1)} fusion(f32[1,7168,512]{1,2,0:T(8,128)S(1)} %get-tuple-element.15, f32[1,7168,128]{1,2,0:T(8,128)S(1)} %copy-done.2, f32[1,128,512]{1,2,0:T(8,128)S(1)} %copy.27), kind=kOutput, calls=%fused_computation.45 | convolution fusion | flops 5641011200 | bytes 18874368 | tf_op jit(solution)/shard_map/edr,edh->erh/dot_general | solution.py:51
  436.0 0.1 copy.20
  436.2 4.5 broadcast_multiply_fusion
  440.7 0.0 reduce-scatter.11.cloned.1.call-update
  440.7 0.0 copy-start.3
  440.7 0.0 reduce-scatter.9.cloned.1.call-start
  440.8 14.0 %fusion.15 = f32[7168,1,128]{0,2,1:T(8,128)} fusion(f32[1,7168,512]{1,2,0:T(8,128)} %copy-done, f32[1,128,512]{1,2,0:T(8,128)S(1)} %copy.27), kind=kOutput, calls=%fused_computation.17 | convolution fusion | flops 5640814592 | bytes 18612224 | tf_op jit(solution)/shard_map/edh,erh->der/dot_general | solution.py:62
  454.8 0.0 reduce-scatter.9.cloned.1.call-update
  454.8 0.0 all-gather.11.cloned.1.call-start
  454.9 56.0 %reduce-scatter.11.cloned.1.call-done = f32[8,128,512]{2,1,0:T(8,128)} async-done(((f32[32,128,512]{2,1,0:T(8,128)}), f32[8,128,512]{2,1,0:T(8,128)}) %reduce-scatter.11.cloned.1.call-update) | async-done | bytes 2097168 | tf_op jit(solution)/shard_map/reduce_scatter | solution.py:54
  510.9 0.0 copy-done.3
  510.9 5.1 fusion.35
  516.0 0.0 all-gather.11.cloned.1.call-update
  516.0 35.0 %all-reduce = (f32[1]{0:T(128)}, f32[1]{0:T(128)}) all-reduce(f32[1]{0:T(128)} %bitcast.30, f32[1]{0:T(128)} %bitcast.29), channel_id=1, replica_groups=mesh['layer'=2,'expert'=4,'col'=4] {'expert','col'}, use_global_device_ids=true, to_apply=%region_9.0 | all-reduce | flops 2 | bytes 16 | tf_op jit(solution)/shard_map/psum | solution.py:78
  551.0 10.2 %copy.31 = f32[32,128,512]{1,0,2:T(8,128)} copy(f32[32,128,512]{2,1,0:T(8,128)} %all-gather.7.cloned.1.call-done) | data formatting | bytes 16777216 | tf_op jit(solution)/shard_map/all_gather | solution.py:77
  561.2 9.0 %convolution_bitcast_fusion = f32[1,32]{1,0:T(1,128)S(1)} fusion(f32[128,512,1]{0,2,1:T(1,128)S(1)} %bitcast.132, f32[32,128,512]{1,0,2:T(8,128)} %copy.31), kind=kOutput, calls=%fused_computation.46 | convolution fusion | flops 25165824 | bytes 8650880 | tf_op jit(solution)/shard_map/krh,erh->ek/dot_general | solution.py:60
  570.2 9.2 %psum.29 = f32[1,32]{1,0:T(1,128)S(1)} all-reduce(f32[1,32]{1,0:T(1,128)S(1)} %convolution_bitcast_fusion), channel_id=1, replica_groups=mesh['layer'=2,'expert'=4,'col'=4] {'col'}, use_global_device_ids=true, to_apply=%region_5.0 | all-reduce | flops 32 | bytes 256 | tf_op jit(solution)/shard_map/psum | solution.py:60
  579.4 1.9 maximum_multiply_fusion
  581.3 0.5 divide_subtract_fusion.1
  581.8 1.2 reduce-scatter.9.cloned.1.call-done
  583.0 0.0 copy-done.6
  583.0 2.2 fusion.56
  585.2 1.2 copy.21
  586.5 56.7 %all-gather.11.cloned.1.call-done = f32[32,128,512]{2,1,0:T(8,128)} async-done(((f32[8,128,512]{2,1,0:T(8,128)}), f32[32,128,512]{2,1,0:T(8,128)}) %all-gather.11.cloned.1.call-update) | async-done | bytes 8388624 | tf_op jit(solution)/shard_map/all_gather | solution.py:77
  643.2 8.4 %copy.37 = f32[32,128,512]{2,1,0:T(8,128)} copy(f32[32,128,512]{2,1,0:T(8,128)} %all-gather.11.cloned.1.call-done) | data formatting | bytes 16777216
  (8 shorter events, 0.0 us)
Async XLA Ops:
  7.2 77.2 %all-gather.5.cloned.1.call-start = ((), (), s32[]{:S(2)}) async-start(), calls=%async_computation.4 | async-start | bytes 4587520 | tf_op jit(solution)/shard_map/all_gather | solution.py:44
  7.9 187.6 %reduce-scatter.7.cloned.1.call-start = ((), (), s32[]{:S(2)}) async-start(), calls=%async_computation.6 | async-start | bytes 10485760 | tf_op jit(solution)/shard_map/reduce_scatter | solution.py:54
  84.4 24.4 %copy-start.4 = (f32[1,7168,128]{2,1,0:T(8,128)S(1)}, f32[1,7168,128]{2,1,0:T(8,128)}, u32[]{:S(2)}) copy-start(f32[1,7168,128]{2,1,0:T(8,128)} %all-gather.5.cloned.1.call-done) | copy-start | bytes 11010052
  103.7 5.2 copy-start.1
  108.8 11.9 %copy-start.7 = (f32[1,32]{1,0:T(1,128)S(1)}, f32[1,32]{1,0:T(1,128)}, u32[]{:S(2)}) copy-start(f32[1,32]{1,0:T(1,128)} %param.7) | copy-start | bytes 388
  125.3 141.0 %reduce-scatter.5.cloned.1.call-start = ((), (), s32[]{:S(2)}) async-start(), calls=%async_computation.5 | async-start | bytes 4587520 | tf_op jit(solution)/shard_map/reduce_scatter | solution.py:61
  139.2 60.9 %copy-start.5 = (f32[1,1792,128]{2,1,0:T(8,128)S(1)}, f32[1,1792,128]{2,1,0:T(8,128)}, u32[]{:S(2)}) copy-start(f32[1,1792,128]{2,1,0:T(8,128)} %param.5) | copy-start | bytes 2752516
  139.3 187.1 %all-gather.7.cloned.1.call-start = ((), (), s32[]{:S(2)}) async-start(), calls=%async_computation.7 | async-start | bytes 10485760 | tf_op jit(solution)/shard_map/all_gather | solution.py:77
  200.1 200.4 %all-gather.9.cloned.1.call-start = ((), (), s32[]{:S(2)}) async-start(), calls=%async_computation.8 | async-start | bytes 4587520 | tf_op jit(solution)/shard_map/all_gather | solution.py:44
  269.0 241.9 %reduce-scatter.11.cloned.1.call-start = ((), (), s32[]{:S(2)}) async-start(), calls=%async_computation.10 | async-start | bytes 10485760 | tf_op jit(solution)/shard_map/reduce_scatter | solution.py:54
  400.4 23.8 %copy-start.2 = (f32[1,7168,128]{1,2,0:T(8,128)S(1)}, f32[1,7168,128]{1,2,0:T(8,128)}, u32[]{:S(2)}) copy-start(f32[1,7168,128]{1,2,0:T(8,128)} %all-gather.9.cloned.1.call-done) | copy-start | bytes 11010052
  419.1 5.2 copy-start
  440.7 70.2 %copy-start.3 = (f32[8,128,512]{2,1,0:T(8,128)S(1)}, f32[8,128,512]{2,1,0:T(8,128)}, u32[]{:S(2)}) copy-start(f32[8,128,512]{2,1,0:T(8,128)} %divide_subtract_fusion) | copy-start | bytes 6291460
  440.7 142.3 %reduce-scatter.9.cloned.1.call-start = ((), (), s32[]{:S(2)}) async-start(), calls=%async_computation.9 | async-start | bytes 4587520 | tf_op jit(solution)/shard_map/reduce_scatter | solution.py:61
  454.8 188.3 %all-gather.11.cloned.1.call-start = ((), (), s32[]{:S(2)}) async-start(), calls=%async_computation.11 | async-start | bytes 10485760 | tf_op jit(solution)/shard_map/all_gather | solution.py:77
  561.2 21.8 %copy-start.6 = (f32[1792,1,128]{0,2,1:T(8,128)S(1)}, f32[1792,1,128]{0,2,1:T(8,128)}, u32[]{:S(2)}) copy-start(f32[1792,1,128]{0,2,1:T(8,128)} %reduce-scatter.5.cloned.1.call-done) | copy-start | bytes 2752516
Sparse Core Ops, SparseCore 0:
  9.5 74.8 all-gather.4
  125.5 69.9 reduce-scatter.6
  197.8 68.5 reduce-scatter.4
  267.8 58.5 all-gather.6
  328.3 72.0 all-gather.8
  440.8 69.9 reduce-scatter.10
  513.2 69.7 reduce-scatter.8
  584.6 58.5 all-gather.10
where the time goes:
time: 664 us; the launch traced here: 659 us
  waiting for transfers between devices  378 us (57%)
  matrix products  132 us (20%)
  blocking collectives  55.8 us (8%)
  local copies, waits for them, and re-layouts  51.6 us (8%)
  other arithmetic  25.9 us (4%)
  between operations  14.5 us (2%)
    all_gather x2, waiting for transfers between devices, shards(): gathered = lax.all_gather(current_factors, 'col', axis=1, tiled=True)  116 us
    reduce_scatter x2, waiting for transfers between devices, shards(): lax.psum_scatter(jnp.einsum('ek,erh->krh', coef_slice, d_pre, precision=H...  112 us
    all_gather x2, waiting for transfers between devices, shards(): current_bases = lax.all_gather(own_bases, 'expert', axis=0, tiled=True)  82.5 us
    reduce_scatter x2, waiting for transfers between devices, shards(): lax.psum_scatter(jnp.einsum('edh,erh->der', gradient, mixed, precision=HI...  67.1 us
    unnamed x21, local copies, waits for them, and re-layouts  40.9 us
    dot_general x2, matrix products, shards(): jnp.einsum('edr,erh->edh', gathered, mixed, precision=HIGHEST)  37.9 us
    psum x1, blocking collectives, shards(): loss_values.append(lax.psum(loss_part, ('expert', 'col')))  35 us
    dot_general x2, matrix products, shards(): jnp.einsum('edh,erh->der', gradient, mixed, precision=HIGHEST)  27.9 us
  transfers between devices with their start and end apart: 8, of which 8 were waited for; matrix products, arithmetic and copies ran while one was open for 18% of the time, Pallas kernels for 0%

commit v1 on v0

v1 whole, which is shorter than its diff:
```python
import jax
import jax.numpy as jnp
from jax import lax
from jax.sharding import PartitionSpec as P

LEARN_RATE = 0.01
BETA_ONE = 0.9
BETA_TWO = 0.999
EPSILON = 0.0001
HIGHEST = lax.Precision.HIGHEST


def adam_first(parameter, g):
    return parameter - LEARN_RATE * g / (jnp.abs(g) + EPSILON)


def adam_second(parameter, g_one, g_two):
    first = (BETA_ONE * (1.0 - BETA_ONE) * g_one + (1.0 - BETA_ONE) * g_two) * (1.0 / (1.0 - BETA_ONE**2))
    second = (
        BETA_TWO * (1.0 - BETA_TWO) * g_one * g_one + (1.0 - BETA_TWO) * g_two * g_two
    ) * (1.0 / (1.0 - BETA_TWO**2))
    return parameter - LEARN_RATE * first / (jnp.sqrt(second) + EPSILON)


def pieces(x, count=3):
    out = []
    for _ in range(count):
        piece = lax.reduce_precision(x, 8, 7)
        out.append(piece.astype(jnp.bfloat16))
        x = x - piece
    return out


def left_dot(target, mixed):
    total = 0.0
    for piece in pieces(mixed):
        total = total + lax.dot_general(
            target, piece, (((1,), (1,)), ((), ())), preferred_element_type=jnp.float32
        )
    return total


def down_dot(full, target):
    r = full.shape[1]
    stacked = jnp.concatenate(pieces(full), axis=1)
    parts = lax.dot_general(
        stacked, target, (((0,), (0,)), ((), ())), preferred_element_type=jnp.float32
    )
    return parts[:r] + parts[r : 2 * r] + parts[2 * r :]


def outer_basis(coef_all, d_pre_all):
    total = coef_all[0][:, None, None] * d_pre_all[0][None]
    for e in range(1, coef_all.shape[0]):
        total = total + coef_all[e][:, None, None] * d_pre_all[e][None]
    return total


def shards(target_weights, factors, bases, coefficients):
    target = target_weights[0]
    own = factors[0]
    experts = lax.axis_size("expert")
    cols = lax.axis_size("col")
    me = lax.axis_index("expert")
    d, h = target.shape[0], target.shape[1] * cols
    k = bases.shape[0]
    scale = 1.0 / h

    coef_all = lax.all_gather(coefficients[0], "expert", axis=0)
    full = lax.all_gather(own, "col", axis=0, tiled=True)
    coef = coefficients[0]

    def mix(c, b):
        return jnp.tanh(jnp.sum(c[:, None, None] * b, axis=0))

    def own_gradient(mixed, rows):
        gram = jnp.dot(mixed, mixed.T, precision=HIGHEST)
        r = gram.shape[0]
        part = left_dot(target, mixed).reshape(cols, -1, r)
        joined = jnp.concatenate([part, jnp.broadcast_to(gram, (cols, r, r))], axis=1)
        summed = lax.psum_scatter(joined, "col", scatter_dimension=0, tiled=False)
        return (jnp.dot(rows, summed[-r:], precision=HIGHEST) - summed[:-r]) * scale

    def pre_gradient(mixed, whole):
        gram = lax.dot_general(whole, whole, (((0,), (0,)), ((), ())), precision=HIGHEST)
        d_mixed = jnp.dot(gram, mixed, precision=HIGHEST) - down_dot(whole, target)
        return d_mixed * scale * (1.0 - mixed * mixed)

    def loss_of(mixed, whole):
        residual = jnp.dot(whole, mixed, precision=HIGHEST) - target.astype(jnp.float32)
        return jnp.sum(residual * residual)

    mixed_one = mix(coef, bases)
    g_factor_one = own_gradient(mixed_one, own)
    d_pre_one = pre_gradient(mixed_one, full)
    d_pre_one_all = lax.all_gather(d_pre_one, "expert", axis=0)
    d_coef_one = jnp.sum(bases * d_pre_one[None], axis=(1, 2))
    g_coef_one = jnp.sum(lax.all_gather(d_coef_one, ("expert", "col"), axis=0).reshape(experts, cols, k), axis=1)
    bases_two = adam_first(bases, outer_basis(coef_all, d_pre_one_all))
    coef_all_two = adam_first(coef_all, g_coef_one)
    coef_two = lax.dynamic_index_in_dim(coef_all_two, me, 0, keepdims=False)
    own_two = adam_first(own, g_factor_one)
    full_two = lax.all_gather(own_two, "col", axis=0, tiled=True)
    loss_one = loss_of(mixed_one, full)

    mixed_two = mix(coef_two, bases_two)
    g_factor_two = own_gradient(mixed_two, own_two)
    d_pre_two = pre_gradient(mixed_two, full_two)
    d_pre_two_all = lax.all_gather(d_pre_two, "expert", axis=0)
    d_coef_two = jnp.sum(bases_two * d_pre_two[None], axis=(1, 2))
    loss_two = loss_of(mixed_two, full_two)
    message = jnp.concatenate([d_coef_two, jnp.stack([loss_one, loss_two])])
    gathered = lax.all_gather(message, ("expert", "col"), axis=0)
    g_coef_two = jnp.sum(gathered.reshape(experts, cols, k + 2), axis=1)
    losses = jnp.sum(g_coef_two[:, k:], axis=0) * (1.0 / (2.0 * experts * d * h))
    coef_all_three = adam_second(coef_all_two, g_coef_one, g_coef_two[:, :k])
    coef_three = lax.dynamic_slice_in_dim(coef_all_three, me, 1, 0)
    bases_three = adam_second(
        bases_two, outer_basis(coef_all, d_pre_one_all), outer_basis(coef_all_two, d_pre_two_all)
    )
    own_three = adam_second(own_two, g_factor_one, g_factor_two)
    return (own_three[None], bases_three, coef_three, losses)


def solution(mesh):
    return jax.shard_map(
        shards,
        mesh=mesh,
        in_specs=(
            P(("layer", "expert"), None, "col"),
            P(("layer", "expert"), "col", None),
            P("layer", None, "col"),
            P(("layer", "expert"), None),
        ),
        out_specs=(
            P(("layer", "expert"), "col", None),
            P("layer", None, "col"),
            P(("layer", "expert"), None),
            P("layer"),
        ),
        check_vma=False,
    )
```

time: 664 us -> 408 us (0.61)
  waiting for transfers between devices: 378 us -> 146 us
  matrix products: 132 us -> 91.4 us
  local copies, waits for them, and re-layouts: 51.6 us -> 28.7 us
  other arithmetic: 25.9 us -> 47.9 us
  blocking collectives: 55.8 us -> 71.5 us
    reduce_scatter x4 -> x2, waiting for transfers between devices: 179 us -> 55.8 us  [own_gradient(): summed = lax.psum_scatter(joined, 'col', scatter_dimension=0, tiled=False)]
    all_gather x4, waiting for transfers between devices: 198 us -> 89.3 us  [the longest x1 60 us: shards(): full = lax.all_gather(own, 'col', axis=0, tiled=True)]
    unnamed x0 -> x2, blocking collectives: none -> 66.3 us
    psum x3 -> x0, blocking collectives: 55.8 us -> none  [the longest x1 35 us: shards(): loss_values.append(lax.psum(loss_part, ('expert', 'col')))]
    dot_general x10 -> x18, matrix products: 132 us -> 91.4 us  [the longest x2 33.6 us: loss_of(): jnp.dot(whole, mixed, precision=HIGHEST) - target.astype(jnp.float32)]
    reduce_sum x0 -> x7, other arithmetic: none -> 33.5 us  [the longest x1 15.4 us: shards(): d_coef_two = jnp.sum(bases_two * d_pre_two[None], axis=(1, 2))]
    unnamed x21 -> x35, local copies, waits for them, and re-layouts: 40.9 us -> 14.6 us
    sub x6 -> x2, other arithmetic: 15 us -> 0.03 us  [the longest x1 0.02 us: adam_second(): return parameter - LEARN_RATE * first / (jnp.sqrt(second) + EPSILON)]
  transfers between devices with their start and end apart: 8 -> 6, of which waited for: 8 -> 3; matrix products, arithmetic and copies ran while one was open for 18% -> 37% of each run, Pallas kernels for 0% -> 0%
where the time goes in v1:
time: 408 us; the launch traced here: 403 us
  waiting for transfers between devices  146 us (36%)
  matrix products  91.4 us (22%)
  blocking collectives  71.5 us (18%)
  other arithmetic  47.9 us (12%)
  local copies, waits for them, and re-layouts  28.7 us (7%)
  between operations  16.1 us (4%)
    unnamed x2, blocking collectives  66.3 us
    all_gather x1, waiting for transfers between devices, shards(): full = lax.all_gather(own, 'col', axis=0, tiled=True)  60 us
    reduce_scatter x2, waiting for transfers between devices, own_gradient(): summed = lax.psum_scatter(joined, 'col', scatter_dimension=0, tiled=False)  55.8 us
    dot_general x2, matrix products, loss_of(): jnp.dot(whole, mixed, precision=HIGHEST) - target.astype(jnp.float32)  33.6 us
    all_gather x1, waiting for transfers between devices, shards(): full_two = lax.all_gather(own_two, 'col', axis=0, tiled=True)  29.2 us
    dot_general x6, matrix products, left_dot(): lax.dot_general(target, piece, (((1,), (1,)), ((), ())), preferred_elemen...  25.8 us
    reduce_sum x1, other arithmetic, shards(): d_coef_two = jnp.sum(bases_two * d_pre_two[None], axis=(1, 2))  15.4 us
    unnamed x35, local copies, waits for them, and re-layouts  14.6 us
  transfers between devices with their start and end apart: 6, of which 3 were waited for; matrix products, arithmetic and copies ran while one was open for 37% of the time, Pallas kernels for 0%

profile of v1, /device:TPU:0, one launch (start us, length us, event | category | flops | bytes accessed | tf_op | source)
XLA Modules:
  0.0 402.6 jit_solution(10426833088106371099)
XLA Ops:
  7.2 0.0 all-gather.13.cloned.1.call-start
  7.2 0.7 all-gather.13.cloned.1.call-update
  7.9 0.0 reduce-scatter.3.cloned.1.call-start
  8.0 4.8 %multiply_reduce_fusion.3 = f32[128,512]{1,0:T(8,128)S(1)} fusion(f32[32,128,512]{2,1,0:T(8,128)} %param.6, f32[32]{0:T(128)} %bitcast.122), kind=kLoop, calls=%fused_computation.24 | loop fusion | flops 4128768 | bytes 8650880 | tf_op jit(solution)/shard_map/reduce_sum | solution.py:74
  12.8 0.6 copy-done
  13.4 2.5 fusion.21
  15.9 2.5 convolution_add_fusion.3
  18.4 2.5 convolution_add_fusion.2
  20.9 0.3 copy.52
  21.2 0.4 fusion.56
  21.6 2.2 pad_maximum_fusion
  23.8 0.0 reduce-scatter.3.cloned.1.call-update
  23.8 0.5 all-gather.15.cloned.1.call-start
  24.4 60.0 %all-gather.13.cloned.1.call-done = f32[1,7168,128]{2,1,0:T(8,128)} async-done(((f32[1,1792,128]{2,1,0:T(8,128)}), f32[1,7168,128]{2,1,0:T(8,128)}) %all-gather.13.cloned.1.call-update) | async-done | bytes 3670032 | tf_op jit(solution)/shard_map/all_gather | solution.py:70
  84.4 9.2 %fusion.38 = f32[128,128]{1,0:T(8,128)S(1)} fusion(f32[1,7168,128]{2,1,0:T(8,128)} %all-gather.13.cloned.1.call-done), kind=kOutput, calls=%fused_computation.63 | convolution fusion | flops 1409286144 | bytes 3735552 | tf_op jit(solution)/shard_map/dot_general | solution.py:85
  93.6 3.1 reduce-precision_convert_fusion.3
  96.8 0.1 slice-done.1
  96.9 3.0 fusion.17
  100.0 1.1 fusion.44
  101.1 0.0 all-gather.15.cloned.1.call-update
  101.1 0.0 all-gather.11.cloned.1.call-start
  101.1 1.5 copy.36
  102.6 55.8 %reduce-scatter.3.cloned.1.call-done = f32[1,1920,128]{1,2,0:T(8,128)} async-done(((f32[4,1920,128]{1,2,0:T(8,128)}), f32[1,1920,128]{1,2,0:T(8,128)}) %reduce-scatter.3.cloned.1.call-update) | async-done | bytes 983056 | tf_op jit(solution)/shard_map/reduce_scatter | solution.py:81
  158.5 3.7 bitcast_subtract_fusion
  162.2 0.0 all-gather.11.cloned.1.call-update
  162.2 0.0 all-gather.17.cloned.1.call-start
  162.3 0.6 dynamic-slice
  163.6 5.2 %all-gather.5 = f32[4,1,32]{2,1,0:T(1,128)S(1)} all-gather(f32[1,1,32]{2,1,0:T(1,128)S(1)} %bitcast.123), channel_id=1, replica_groups=mesh['layer'=2,'expert'=4,'col'=4] {'expert'}, dimensions={0}, use_global_device_ids=true | all-gather | bytes 640 | tf_op jit(solution)/shard_map/all_gather | solution.py:69
  168.8 4.2 %multiply_reduce_fusion.2 = f32[32]{0:T(128)S(1)} fusion(f32[32,128,512]{2,1,0:T(8,128)} %param.6, f32[128,512]{1,0:T(8,128)S(1)} %copy-done.5), kind=kLoop, calls=%fused_computation.23 | loop fusion | flops 4194272 | bytes 8650880 | tf_op jit(solution)/shard_map/reduce_sum | solution.py:97
  173.0 0.2 dynamic-update-slice
  173.2 34.5 %all-reduce = f32[512]{0:T(512)S(1)} all-reduce(f32[512]{0:T(512)S(1)} %dynamic-update-slice), channel_id=3, replica_groups=mesh['layer'=2,'expert'=4,'col'=4] {'expert','col'}, use_global_device_ids=true, to_apply=%add | all-reduce | flops 512 | bytes 4096
  207.7 0.1 reshape.38
  207.9 0.0 all-gather.15.cloned.1.call-done
  207.9 1.4 fusion.69
  209.3 0.0 slice-start.3
  209.4 9.0 %multiply_reduce_fusion.1 = (f32[128,512]{1,0:T(8,128)S(1)}, f32[32,128,512]{2,1,0:T(8,128)}) fusion(f32[32]{0:T(128)S(1)} %get-tuple-element.42, f32[32,128,512]{2,1,0:T(8,128)} %param.6, f32[128,512]{1,0:T(8,128)S(1)} %get-tuple-element.37, f32[32]{0:T(128)S(1)} %get-tuple-element.44, f32[128,512]{1,0:T(8,128)S(1)} %get-tuple-element.35, ...), kind=kLoop, calls=%fused_computation.20 | loop fusion | flops 29294592 | bytes 18088576 | tf_op jit(solution)/shard_map/reduce_sum | solution.py:74
  218.4 4.3 %fusion.15 = f32[128,7168]{1,0:T(8,128)} fusion(bf16[1,7168,512]{2,1,0:T(8,128)(2,1)S(1)} %bitcast.116, f32[128,512]{1,0:T(8,128)S(1)} %get-tuple-element.20), kind=kOutput, calls=%fused_computation.29 | convolution fusion | flops 939655168 | bytes 11272192 | tf_op jit(solution)/shard_map/dot_general | solution.py:37
  222.6 29.2 %all-gather.11.cloned.1.call-done = f32[7168,128]{0,1:T(8,128)} async-done(((f32[1792,128]{0,1:T(8,128)}), f32[7168,128]{0,1:T(8,128)}) %all-gather.11.cloned.1.call-update) | async-done | bytes 3670032 | tf_op jit(solution)/shard_map/all_gather | solution.py:103
  251.9 2.8 reduce-precision_convert_fusion.1
  254.7 6.3 %fusion.11 = f32[384,512]{1,0:T(8,128)S(1)} fusion(bf16[1,7168,512]{2,1,0:T(8,128)(2,1)} %param.4, bf16[7168,128]{0,1:T(8,128)(2,1)S(1)} %get-tuple-element.25, bf16[7168,128]{0,1:T(8,128)(2,1)S(1)} %get-tuple-element.26, bf16[7168,128]{0,1:T(8,128)(2,1)S(1)} %get-tuple-element.24), kind=kOutput, calls=%fused_computation.25 | convolution fusion | flops 2835087360 | bytes 13631488 | tf_op jit(solution)/shard_map/dot_general | solution.py:46
  261.0 3.0 fusion.70
  264.0 1.1 fusion.42
  265.2 0.0 all-gather.17.cloned.1.call-update
  265.2 0.4 reduce-scatter.5.cloned.1.call-start
  265.6 6.6 %convolution_add_fusion.1 = f32[128,7168]{1,0:T(8,128)S(1)} fusion(f32[128,7168]{1,0:T(8,128)} %fusion.15, bf16[1,7168,512]{2,1,0:T(8,128)(2,1)} %param.4, f32[128,512]{1,0:T(8,128)S(1)} %get-tuple-element.20), kind=kOutput, calls=%fused_computation.10 | convolution fusion | flops 940703744 | bytes 14942208 | tf_op jit(solution)/shard_map/dot_general | solution.py:37
  272.3 7.4 %fusion.4 = f32[7168,128]{0,1:T(8,128)} fusion(f32[128,7168]{1,0:T(8,128)S(1)} %convolution_add_fusion.1, bf16[1,7168,512]{2,1,0:T(8,128)(2,1)} %param.4, f32[128,512]{1,0:T(8,128)S(1)} %get-tuple-element.20), kind=kOutput, calls=%fused_computation.9 | convolution fusion | flops 940834816 | bytes 14942208 | tf_op jit(solution)/shard_map/dot_general | solution.py:37
  279.7 5.3 %copy.40 = f32[7168,128]{1,0:T(8,128)} copy(f32[7168,128]{0,1:T(8,128)} %fusion.4) | data formatting | bytes 7340032 | tf_op jit(solution)/shard_map/add | solution.py:37
  284.9 5.2 %copy.42 = f32[4,1792,128]{1,2,0:T(8,128)} copy(f32[4,1792,128]{2,1,0:T(8,128)} %bitcast.118) | data formatting | bytes 7340032 | tf_op jit(solution)/shard_map/reshape | solution.py:79
  290.1 0.4 fusion.52
  290.5 4.3 %pad_maximum_fusion.1 = f32[4,1920,128]{1,2,0:T(8,128)} fusion(f32[4,128,128]{1,2,0:T(8,128)S(1)} %broadcast_in_dim.16, f32[4,1792,128]{1,2,0:T(8,128)} %copy.42), kind=kLoop, calls=%fused_computation.56 | loop fusion | flops 983040 | bytes 7864320 | tf_op jit(solution)/shard_map/concatenate | solution.py:80
  294.8 0.0 reduce-scatter.5.cloned.1.call-update
  294.9 10.2 %copy.37 = bf16[1,7168,512]{1,2,0:T(8,128)(2,1)} copy(bf16[1,7168,512]{2,1,0:T(8,128)(2,1)} %param.4) | data formatting | bytes 14680064 | tf_op args[0]
  305.9 18.1 %fusion.1 = f32[]{:T(128)} fusion(bf16[1,7168,512]{1,2,0:T(8,128)(2,1)} %copy.37, f32[1,7168,128]{2,1,0:T(8,128)} %all-gather.13.cloned.1.call-done, f32[128,512]{1,0:T(8,128)S(1)} %multiply_reduce_fusion.3), kind=kOutput, calls=%fused_computation.3 | convolution fusion | flops 5651824640 | bytes 11272196 | tf_op jit(solution)/shard_map/dot_general | solution.py:90
  324.0 15.4 %fusion.3 = f32[]{:T(128)} fusion(f32[7168,128]{0,1:T(8,128)S(1)} %copy-done.2, bf16[1,7168,512]{1,2,0:T(8,128)(2,1)S(1)} %copy-done.3, f32[128,512]{1,0:T(8,128)S(1)} %get-tuple-element.20), kind=kOutput, calls=%fused_computation.5 | convolution fusion | flops 5651824640 | bytes 11272196 | tf_op jit(solution)/shard_map/dot_general | solution.py:90
  339.5 1.3 fusion.68
  340.8 15.4 %multiply_reduce_fusion = (f32[32]{0:T(128)S(1)}, f32[32,128,512]{2,1,0:T(8,128)}) fusion(f32[32,128,512]{2,1,0:T(8,128)} %get-tuple-element.21, f32[128,512]{1,0:T(8,128)S(1)} %copy-done.4, f32[128,512]{1,0:T(8,128)S(1)} %get-tuple-element.33, f32[32]{0:T(128)S(1)} %get-tuple-element.39, f32[128,512]{1,0:T(8,128)S(1)} %get-tuple-element.31, ...), kind=kLoop, calls=%fused_computation.19 | loop fusion | flops 60817376 | bytes 19137664 | tf_op jit(solution)/shard_map/reduce_sum | solution.py:110
  356.1 1.4 maximum_dynamic-update-slice_fusion
  357.6 31.8 %all-reduce.1 = f32[544]{0:T(1024)S(1)} all-reduce(f32[544]{0:T(1024)S(1)} %maximum_dynamic-update-slice_fusion), channel_id=6, replica_groups=mesh['layer'=2,'expert'=4,'col'=4] {'expert','col'}, use_global_device_ids=true, to_apply=%add.1 | all-reduce | flops 544 | bytes 4352
  389.3 0.1 reshape.40
  389.5 0.5 constant_dynamic-slice_fusion
  390.0 0.1 slice_reduce_fusion
  390.1 0.5 broadcast_multiply_fusion
  390.6 3.7 subtract_bitcast_fusion
  394.4 1.2 copy.45
  (39 shorter events, 0.2 us)
Async XLA Ops:
  7.2 77.2 %all-gather.13.cloned.1.call-start = ((), (), s32[]{:S(2)}) async-start(), calls=%async_computation.5 | async-start | bytes 4587520 | tf_op jit(solution)/shard_map/all_gather | solution.py:70
  7.9 150.6 %reduce-scatter.3.cloned.1.call-start = ((), (), s32[]{:S(2)}) async-start(), calls=%async_computation.2 | async-start | bytes 4915200 | tf_op jit(solution)/shard_map/reduce_scatter | solution.py:81
  7.9 5.5 %copy-start = (bf16[1,7168,512]{2,1,0:T(8,128)(2,1)S(1)}, bf16[1,7168,512]{2,1,0:T(8,128)(2,1)}, u32[]{:S(2)}) copy-start(bf16[1,7168,512]{2,1,0:T(8,128)(2,1)} %param.4) | copy-start | bytes 22020100
  23.8 72.9 %slice-start = ((s8[7340032]{0:T(1024)(128)(4,1)}), s8[3145728]{0:T(1024)(128)(4,1)S(1)}, s32[]{:S(2)}) async-start(s8[7340032]{0:T(1024)(128)(4,1)} %bitcast.113), calls=%async_computation.8 | async-start | bytes 6291456
  23.8 184.1 %all-gather.15.cloned.1.call-start = ((), (), s32[]{:S(2)}) async-start(), calls=%async_computation.6 | async-start | bytes 1310720 | tf_op jit(solution)/shard_map/all_gather | solution.py:96
  93.6 3.3 slice-start.1
  99.9 62.4 %copy-start.9 = (u32[32]{0:T(128)S(1)}, u32[32]{0:T(128)}, u32[]{:S(2)}) copy-start(u32[32]{0:T(128)} %constant.72) | copy-start | bytes 388
  100.0 63.6 %copy-start.8 = (f32[1,32]{1,0:T(1,128)S(1)}, f32[1,32]{1,0:T(1,128)}, u32[]{:S(2)}) copy-start(f32[1,32]{1,0:T(1,128)} %param.7) | copy-start | bytes 388
  101.1 67.7 %copy-start.5 = (f32[128,512]{1,0:T(8,128)S(1)}, f32[128,512]{1,0:T(8,128)}, u32[]{:S(2)}) copy-start(f32[128,512]{1,0:T(8,128)} %fusion.44) | copy-start | bytes 786436
  101.1 150.8 %all-gather.11.cloned.1.call-start = ((), (), s32[]{:S(2)}) async-start(), calls=%async_computation.4 | async-start | bytes 4587520 | tf_op jit(solution)/shard_map/all_gather | solution.py:103
  102.6 105.2 %copy-start.6 = (f32[1,1792,128]{1,2,0:T(8,128)}, f32[1,1792,128]{1,2,0:T(8,128)S(1)}, u32[]{:S(2)}) copy-start(f32[1,1792,128]{1,2,0:T(8,128)S(1)} %copy.36) | copy-start | bytes 2752516
  162.2 177.2 %all-gather.17.cloned.1.call-start = ((), (), s32[]{:S(2)}) async-start(), calls=%async_computation.7 | async-start | bytes 1310720 | tf_op jit(solution)/shard_map/all_gather | solution.py:109
  207.9 10.4 %slice-start.2 = ((s8[7340032]{0:T(1024)(128)(4,1)}), s8[4194304]{0:T(1024)(128)(4,1)S(1)}, s32[]{:S(2)}) async-start(s8[7340032]{0:T(1024)(128)(4,1)} %bitcast.115), calls=%async_computation.10 | async-start | bytes 8388608
  209.3 9.0 %slice-start.3 = ((s8[7340032]{0:T(1024)(128)(4,1)}), s8[3145728]{0:T(1024)(128)(4,1)S(1)}, s32[]{:S(2)}) async-start(s8[7340032]{0:T(1024)(128)(4,1)} %bitcast.115), calls=%async_computation.11 | async-start | bytes 6291456
  254.7 6.4 %copy-start.1 = (f32[7168,128]{0,1:T(8,128)S(1)}, f32[7168,128]{0,1:T(8,128)}, u32[]{:S(2)}) copy-start(f32[7168,128]{0,1:T(8,128)} %all-gather.11.cloned.1.call-done) | copy-start | bytes 11010052
  265.2 125.4 %reduce-scatter.5.cloned.1.call-start = ((), (), s32[]{:S(2)}) async-start(), calls=%async_computation.3 | async-start | bytes 4915200 | tf_op jit(solution)/shard_map/reduce_scatter | solution.py:81
  305.1 18.9 %copy-start.2 = (f32[7168,128]{0,1:T(8,128)S(1)}, f32[7168,128]{0,1:T(8,128)}, u32[]{:S(2)}) copy-start(f32[7168,128]{0,1:T(8,128)} %all-gather.11.cloned.1.call-done) | copy-start | bytes 11010052
  305.1 18.9 %copy-start.3 = (bf16[1,7168,512]{1,2,0:T(8,128)(2,1)S(1)}, bf16[1,7168,512]{1,2,0:T(8,128)(2,1)}, u32[]{:S(2)}) copy-start(bf16[1,7168,512]{1,2,0:T(8,128)(2,1)} %copy.37) | copy-start | bytes 22020100
  324.0 16.7 %copy-start.4 = (f32[128,512]{1,0:T(8,128)S(1)}, f32[128,512]{1,0:T(8,128)}, u32[]{:S(2)}) copy-start(f32[128,512]{1,0:T(8,128)} %fusion.42) | copy-start | bytes 786436
  340.8 49.9 %copy-start.7 = (f32[1,1792,128]{1,2,0:T(8,128)S(1)}, f32[1,1792,128]{1,2,0:T(8,128)}, u32[]{:S(2)}) copy-start(f32[1,1792,128]{1,2,0:T(8,128)} %copy-done.6) | copy-start | bytes 2752516
Sparse Core Ops, SparseCore 0:
  9.5 74.8 all-gather.12
  87.3 71.1 reduce-scatter.2
  160.1 17.1 all-gather.14
  179.2 72.6 all-gather.10
  265.3 15.3 all-gather.16
  295.0 71.6 reduce-scatter.4

commit v2 on v0

v2 whole, which is shorter than its diff:
```python
import functools

import jax
import jax.numpy as jnp
from jax import lax
from jax.experimental import pallas as pl
from jax.experimental.pallas import tpu as pltpu
from jax.sharding import PartitionSpec as P

LEARN_RATE = 0.01
BETA_ONE = 0.9
BETA_TWO = 0.999
EPSILON = 0.0001
HIGHEST = lax.Precision.HIGHEST
MESH = pl.DeviceIdType.MESH
F32 = jnp.float32
BF16 = jnp.bfloat16


def adam_first(parameter, g):
    return parameter - LEARN_RATE * g / (jnp.abs(g) + EPSILON)


def adam_second(parameter, g_one, g_two):
    first = (BETA_ONE * (1.0 - BETA_ONE) * g_one + (1.0 - BETA_ONE) * g_two) * (1.0 / (1.0 - BETA_ONE**2))
    second = (
        BETA_TWO * (1.0 - BETA_TWO) * g_one * g_one + (1.0 - BETA_TWO) * g_two * g_two
    ) * (1.0 / (1.0 - BETA_TWO**2))
    return parameter - LEARN_RATE * first / (jnp.sqrt(second) + EPSILON)


def pieces(x, count=3):
    out = []
    for _ in range(count):
        piece = x.astype(BF16)
        out.append(piece)
        x = x - piece.astype(F32)
    return out


def contract(a, b, dims):
    return lax.dot_general(a, b, (dims, ((), ())), preferred_element_type=F32)


def fold(x, r):
    return x[:, :r] + x[:, r : 2 * r] + x[:, 2 * r :]


def fold_rows(x, r):
    return x[:r] + x[r : 2 * r] + x[2 * r :]


def kernel(
    n, experts, t_hbm, f_hbm, b_hbm, c_in, f_out, b_out, c_out, l_out,
    target, bases, full, part, landed, d_pre, c_one, c_two, d_coef, loss_in, g_one, gram_sum,
    mixed, mixed_cut, loss_sum, load_sem, ag_send, ag_recv, rs_send, rs_recv, ex_send, ex_recv, co_send, co_recv,
):
    me = lax.axis_index("col")
    mine = lax.axis_index("expert")
    rows, r = f_out.shape
    d, hl = target.shape
    k_count = bases.shape[0]
    scale = 1.0 / (hl * n)
    table = experts * k_count

    loads = [
        pltpu.make_async_copy(f_hbm, full.at[0, pl.ds(pl.multiple_of(me * rows, 8), rows)], load_sem.at[0]),
        pltpu.make_async_copy(b_hbm, bases, load_sem.at[1]),
        pltpu.make_async_copy(t_hbm, target, load_sem.at[2]),
        pltpu.make_async_copy(c_in, c_one.at[mine], load_sem.at[3]),
    ]
    for load in loads:
        load.start()
    barrier = pltpu.get_barrier_semaphore()
    for off in range(1, n):
        pl.semaphore_signal(barrier, inc=1, device_id={"col": lax.rem(me + off, n)}, device_id_type=MESH)
    for off in range(1, experts):
        pl.semaphore_signal(barrier, inc=1, device_id={"expert": lax.rem(mine + off, experts)}, device_id_type=MESH)
    pl.semaphore_wait(barrier, n + experts - 2)

    def shard_copy(it, way, s, shard):
        place = full.at[it, pl.ds(pl.multiple_of(shard * rows, 8), rows)]
        return pltpu.make_async_remote_copy(
            src_ref=place, dst_ref=place, send_sem=ag_send.at[it, way, s], recv_sem=ag_recv.at[it, way, s],
            device_id={"col": me + 1 - 2 * way}, device_id_type=MESH,
        )

    def gather_step(it, t):
        for way in range(2):
            shard = me - t * (1 - 2 * way)
            after = me + 1 - 2 * way
            inside = (shard >= 0) & (shard < n)

            if t >= 1:
                @pl.when(inside)
                def _():
                    shard_copy(it, way, t - 1, shard).wait_recv()

            if t <= n - 2:
                @pl.when(inside & (after >= 0) & (after < n))
                def _():
                    shard_copy(it, way, t, shard).start()

    def gather_sent(it):
        for way in range(2):
            for s in range(n - 1):
                shard = me - s * (1 - 2 * way)
                after = me + 1 - 2 * way

                @pl.when((shard >= 0) & (shard < n) & (after >= 0) & (after < n))
                def _():
                    shard_copy(it, way, s, shard).wait_send()

    def part_copy(it, way, s, j):
        return pltpu.make_async_remote_copy(
            src_ref=part.at[j], dst_ref=landed.at[way, s], send_sem=rs_send.at[it, way, s],
            recv_sem=rs_recv.at[it, way, s], device_id={"col": me + 1 - 2 * way}, device_id_type=MESH,
        )

    def scatter_step(it, t):
        for way in range(2):
            place = me if way == 0 else n - 1 - me
            s = t - place
            j = n - 1 - s if way == 0 else s

            @pl.when((place > 0) & (s >= 0))
            def _():
                part_copy(it, way, s, j).wait_recv()
                part[j] = part[j] + landed[way, s]

            if t <= n - 2:
                @pl.when(s >= 0)
                def _():
                    part_copy(it, way, s, j).start()

    def scatter_sent(it):
        for way in range(2):
            place = me if way == 0 else n - 1 - me
            for t in range(n - 1):
                s = t - place

                @pl.when(s >= 0)
                def _():
                    part_copy(it, way, s, n - 1 - s if way == 0 else s).wait_send()

    def expert_copy(ref, kind, off):
        place = ref.at[mine]
        return pltpu.make_async_remote_copy(
            src_ref=place, dst_ref=place, send_sem=ex_send.at[kind, off - 1], recv_sem=ex_recv.at[kind, off - 1],
            device_id={"expert": lax.rem(mine + off, experts)}, device_id_type=MESH,
        )

    def expert_start(ref, kind):
        for off in range(1, experts):
            expert_copy(ref, kind, off).start()

    def expert_wait(ref, kind):
        for off in range(1, experts):
            expert_copy(ref, kind, off).wait()

    def coef_copy(it, off):
        place = d_coef.at[it, me]
        return pltpu.make_async_remote_copy(
            src_ref=place, dst_ref=place, send_sem=co_send.at[it, off - 1], recv_sem=co_recv.at[it, off - 1],
            device_id={"col": lax.rem(me + off, n)}, device_id_type=MESH,
        )

    def mix(c_ref, b_ref):
        for q in range(0, hl, 128):
            def add(k, total):
                return total + c_ref[mine, pl.ds(k, 1), :] * b_ref[k, :, q : q + 128]

            mixed[:, q : q + 128] = jnp.tanh(lax.fori_loop(0, k_count, add, jnp.zeros((r, 128), F32)))
        for i, piece in enumerate(pieces(mixed[...])):
            mixed_cut[i * r : (i + 1) * r, :] = piece

    step = rows // 4 if (rows // 4) % 16 == 0 else rows

    def project():
        cut = mixed_cut[...]
        gram = fold_rows(fold(contract(cut, cut, ((1,), (1,))), r), r)
        for j in range(n):
            part[j, rows : rows + r, :] = gram

        def block(i, carry):
            at = pl.ds(pl.multiple_of(i * step, 16), step)
            value = fold(contract(target[at, :], mixed_cut[...], ((1,), (1,))), r)
            j = i // (rows // step)
            part[j, pl.ds(pl.multiple_of((i - j * (rows // step)) * step, 8), step), :] = value
            return carry

        lax.fori_loop(0, d // step, block, 0)

    def absorb(it, shard):
        half = rows // 2

        def block(i, carry):
            at = pl.ds(pl.multiple_of(shard * rows + i * half, 16), half)
            cut = jnp.concatenate(pieces(full[it, at, :]), axis=1)
            gram_sum[...] += contract(cut, jnp.concatenate([target[at, :], cut], axis=1), ((0,), (0,)))
            return carry

        lax.fori_loop(0, 2, block, 0)

    def absorb_step(it, t):
        if t == 0:
            gram_sum[...] = jnp.zeros_like(gram_sum)
            absorb(it, me)
        else:
            for way in range(2):
                shard = me - t * (1 - 2 * way)

                @pl.when((shard >= 0) & (shard < n))
                def _():
                    absorb(it, shard)

    def pre_gradient(it):
        total = fold_rows(gram_sum[...], r)
        gram = fold(total[:, hl:], r)
        now = mixed[...]
        d_mixed = jnp.dot(gram, now, precision=HIGHEST, preferred_element_type=F32) - total[:, :hl]
        d_pre[it, mine] = d_mixed * scale * (1.0 - now * now)

    def loss_of(it):
        loss_sum[...] = jnp.zeros_like(loss_sum)

        def block(i, carry):
            at = pl.ds(pl.multiple_of(i * 256, 256), 256)
            one, two = pieces(full[it, at, :], 2)
            wide = jnp.concatenate([one, two, one, two], axis=1)
            tall = jnp.concatenate(
                [mixed_cut[:r], mixed_cut[:r], mixed_cut[r : 2 * r], mixed_cut[r : 2 * r]], axis=0
            )
            residual = contract(wide, tall, ((1,), (0,))) - target[at, :].astype(F32)
            loss_sum[...] += jnp.sum((residual * residual).reshape(32, 8, hl), axis=0)
            return carry

        lax.fori_loop(0, d // 256, block, 0)
        total = loss_sum[:, 0:128]
        for q in range(128, hl, 128):
            total = total + loss_sum[:, q : q + 128]
        loss_in[mine, it * 8 : it * 8 + 8, :] = total

    def combine(c_ref, it, k, q):
        total = c_ref[0, pl.ds(k, 1), :] * d_pre[it, 0, :, q : q + 128]
        for e in range(1, experts):
            total = total + c_ref[e, pl.ds(k, 1), :] * d_pre[it, e, :, q : q + 128]
        return total

    def coef_rows(it, k, q, values):
        for e in range(experts):
            row = jnp.sum(values * d_pre[it, e, :, q : q + 128], axis=0, keepdims=True)
            at = (it, me, pl.ds(e * k_count + k, 1), slice(None))
            if q == 0:
                d_coef[at] = row
            else:
                d_coef[at] = d_coef[at] + row

    def coef_sum(it):
        total = d_coef[it, 0]
        for c in range(1, n):
            total = total + d_coef[it, c]
        return jnp.broadcast_to(jnp.sum(total, axis=1, keepdims=True), total.shape)

    def factor_gradient(i):
        at = pl.ds(pl.multiple_of(i * step, 8), step)
        before = full[0, pl.ds(pl.multiple_of(me * rows + i * step, 8), step), :]
        return at, before

    loads[0].wait()
    gather_step(0, 0)
    loads[3].wait()
    expert_start(c_one, 0)
    loads[1].wait()
    mix(c_one, bases)
    loads[2].wait()
    project()
    scatter_step(0, 0)
    absorb_step(0, 0)
    for t in range(1, n):
        gather_step(0, t)
        if t < n - 1:
            scatter_step(0, t)
        absorb_step(0, t)
    pre_gradient(0)
    expert_wait(c_one, 0)
    expert_start(d_pre.at[0], 1)
    scatter_step(0, n - 1)

    def factor_one(i, carry):
        at, before = factor_gradient(i)
        gram = part[me, rows : rows + r, :]
        g = (jnp.dot(before, gram, precision=HIGHEST, preferred_element_type=F32) - part[me, at, :]) * scale
        g_one[at, :] = g
        full[1, pl.ds(pl.multiple_of(me * rows + i * step, 8), step), :] = adam_first(before, g)
        return carry

    lax.fori_loop(0, rows // step, factor_one, 0)
    gather_step(1, 0)
    loss_of(0)
    scatter_sent(0)
    gather_sent(0)
    expert_wait(d_pre.at[0], 1)

    def bases_one(k, carry):
        for q in range(0, hl, 128):
            values = bases[k, :, q : q + 128]
            b_out[k, :, q : q + 128] = adam_first(values, combine(c_one, 0, k, q))
            coef_rows(0, k, q, values)
        return carry

    lax.fori_loop(0, k_count, bases_one, 0)
    d_coef[0, me, table : table + 8, :] = jnp.zeros((8, 128), F32)
    for off in range(1, n):
        coef_copy(0, off).start()
    absorb_step(1, 0)
    for off in range(1, n):
        coef_copy(0, off).wait()
    c_two[...] = adam_first(c_one[...], coef_sum(0)[:table].reshape(experts, k_count, 128))
    mix(c_two, b_out)
    if n > 1:
        gather_step(1, 1)
    project()
    scatter_step(1, 0)
    absorb_step(1, 1)
    for t in range(2, n):
        gather_step(1, t)
        scatter_step(1, t - 1)
        absorb_step(1, t)
    pre_gradient(1)
    expert_start(d_pre.at[1], 2)
    loss_of(1)
    expert_start(loss_in, 3)
    expert_wait(d_pre.at[1], 2)
    expert_wait(loss_in, 3)

    def bases_two(k, carry):
        for q in range(0, hl, 128):
            values = b_out[k, :, q : q + 128]
            coef_rows(1, k, q, values)
            b_out[k, :, q : q + 128] = adam_second(values, combine(c_one, 0, k, q), combine(c_two, 1, k, q))
        return carry

    lax.fori_loop(0, k_count, bases_two, 0)
    losses = loss_in[0]
    for e in range(1, experts):
        losses = losses + loss_in[e]
    for it in range(2):
        d_coef[1, me, table + it : table + it + 1, :] = jnp.sum(losses[it * 8 : it * 8 + 8], axis=0, keepdims=True)
    d_coef[1, me, table + 2 : table + 8, :] = jnp.zeros((6, 128), F32)
    for off in range(1, n):
        coef_copy(1, off).start()
    scatter_step(1, n - 1)

    def factor_two(i, carry):
        at, _ = factor_gradient(i)
        before = full[1, pl.ds(pl.multiple_of(me * rows + i * step, 8), step), :]
        gram = part[me, rows : rows + r, :]
        g = (jnp.dot(before, gram, precision=HIGHEST, preferred_element_type=F32) - part[me, at, :]) * scale
        f_out[at, :] = adam_second(before, g_one[at, :], g)
        return carry

    lax.fori_loop(0, rows // step, factor_two, 0)
    for off in range(1, n):
        coef_copy(1, off).wait()
    total = coef_sum(1)
    l_out[...] = total[table : table + 8]
    first = coef_sum(0)[:table].reshape(experts, k_count, 128)
    c_two[...] = adam_second(c_two[...], first, total[:table].reshape(experts, k_count, 128))
    c_out[...] = c_two[mine]
    scatter_sent(1)
    gather_sent(1)


def shards(target_weights, factors, bases, coefficients):
    n, experts = lax.axis_size("col"), lax.axis_size("expert")
    _, d, hl = target_weights.shape
    _, rows, r = factors.shape
    k = bases.shape[0]
    anywhere = pl.BlockSpec(memory_space=pl.ANY)
    local = pl.BlockSpec(memory_space=pltpu.VMEM)
    dma = pltpu.SemaphoreType.DMA
    new_factors, new_bases, new_coef, losses = pl.pallas_call(
        functools.partial(kernel, n, experts),
        out_shape=(
            jax.ShapeDtypeStruct((rows, r), F32),
            jax.ShapeDtypeStruct(bases.shape, F32),
            jax.ShapeDtypeStruct((k, 128), F32),
            jax.ShapeDtypeStruct((8, 128), F32),
        ),
        in_specs=[anywhere, anywhere, anywhere, anywhere],
        out_specs=(local, local, local, local),
        scratch_shapes=[
            pltpu.VMEM((d, hl), BF16),
            pltpu.VMEM(bases.shape, F32),
            pltpu.VMEM((2, d, r), F32),
            pltpu.VMEM((n, rows + r, r), F32),
            pltpu.VMEM((2, n - 1, rows + r, r), F32),
            pltpu.VMEM((2, experts, r, hl), F32),
            pltpu.VMEM((experts, k, 128), F32),
            pltpu.VMEM((experts, k, 128), F32),
            pltpu.VMEM((2, n, experts * k + 8, 128), F32),
            pltpu.VMEM((experts, 16, 128), F32),
            pltpu.VMEM((rows, r), F32),
            pltpu.VMEM((3 * r, hl + 3 * r), F32),
            pltpu.VMEM((r, hl), F32),
            pltpu.VMEM((3 * r, hl), BF16),
            pltpu.VMEM((8, hl), F32),
            dma((4,)),
            dma((2, 2, n - 1)),
            dma((2, 2, n - 1)),
            dma((2, 2, n - 1)),
            dma((2, 2, n - 1)),
            dma((4, experts - 1)),
            dma((4, experts - 1)),
            dma((2, n - 1)),
            dma((2, n - 1)),
        ],
        compiler_params=pltpu.CompilerParams(
            collective_id=0, has_side_effects=True, vmem_limit_bytes=66000000
        ),
    )(target_weights[0], factors[0], bases, jnp.broadcast_to(coefficients[0][:, None], (k, 128)))
    total = losses[:2, 0]
    return (new_factors[None], new_bases, new_coef[:, 0][None], total * (1.0 / (2.0 * experts * d * hl * n)))


def solution(mesh):
    return jax.shard_map(
        shards,
        mesh=mesh,
        in_specs=(
            P(("layer", "expert"), None, "col"),
            P(("layer", "expert"), "col", None),
            P("layer", None, "col"),
            P(("layer", "expert"), None),
        ),
        out_specs=(
            P(("layer", "expert"), "col", None),
            P("layer", None, "col"),
            P(("layer", "expert"), None),
            P("layer"),
        ),
        check_vma=False,
    )
```

time: 664 us -> 228 us (0.34)
  waiting for transfers between devices: 378 us -> 0 us
  Pallas kernels: 0 us -> 213 us
  matrix products: 132 us -> 0 us
  blocking collectives: 55.8 us -> 0 us
  local copies, waits for them, and re-layouts: 51.6 us -> 13.2 us
  other arithmetic: 25.9 us -> 1.3 us
  between operations: 14.5 us -> 0.64 us
    pallas_call x0 -> x1, Pallas kernels: none -> 213 us  [shards(): pl.pallas_call(functools.partial(kernel, n, experts), out_shape=(jax.Shap...]
    all_gather x4 -> x0, waiting for transfers between devices: 198 us -> none  [the longest x2 116 us: shards(): gathered = lax.all_gather(current_factors, 'col', axis=1, tiled=True)]
    reduce_scatter x4 -> x0, waiting for transfers between devices: 179 us -> none  [the longest x2 112 us: shards(): lax.psum_scatter(jnp.einsum('ek,erh->krh', coef_slice, d_pre, precision=H...]
    dot_general x10 -> x0, matrix products: 132 us -> none  [the longest x2 37.9 us: shards(): jnp.einsum('edr,erh->edh', gathered, mixed, precision=HIGHEST)]
    psum x3 -> x0, blocking collectives: 55.8 us -> none  [the longest x1 35 us: shards(): loss_values.append(lax.psum(loss_part, ('expert', 'col')))]
    unnamed x21 -> x2, local copies, waits for them, and re-layouts: 40.9 us -> 10.5 us
    sub x6 -> x0, other arithmetic: 15 us -> none  [adam_update(): parameter - LEARN_RATE * first_hat / (jnp.sqrt(second_hat) + EPSILON)]
    all_gather x1 -> x0, local copies, waits for them, and re-layouts: 10.2 us -> none  [shards(): current_bases = lax.all_gather(own_bases, 'expert', axis=0, tiled=True)]
  transfers between devices with their start and end apart: 8 -> 0, of which waited for: 8 -> 0; matrix products, arithmetic and copies ran while one was open for 18% -> 0% of each run, Pallas kernels for 0% -> 0%
where the time goes in v2:
time: 228 us
  Pallas kernels  213 us (93%)
  local copies, waits for them, and re-layouts  13.2 us (6%)
    pallas_call x1, Pallas kernels, shards(): pl.pallas_call(functools.partial(kernel, n, experts), out_shape=(jax.Shap...  213 us
    unnamed x2, local copies, waits for them, and re-layouts  10.5 us

profile of v2, /device:TPU:0, one launch (start us, length us, event | category | flops | bytes accessed | tf_op | source)
XLA Modules:
  0.0 228.1 jit_solution(15084583766773031140)
XLA Ops:
  0.6 1.3 broadcast_in_dim.11.c_in
  2.0 212.9 %shard_map.75 = (f32[1792,128]{1,0:T(8,128)}, f32[32,128,512]{2,1,0:T(8,128)}, f32[32,128]{1,0:T(8,128)}, f32[8,128]{1,0:T(8,128)}) custom-call(bf16[7168,512]{1,0:T(8,128)(2,1)} %bitcast.5, f32[1792,128]{1,0:T(8,128)} %bitcast.7, f32[32,128,512]{2,1,0:T(8,128)} %b_hbm.1, f32[32,128]{1,0:T(8,128)} %broadcast_in_dim.11.c_in), custom_call_target="tpu_custom_call" | custom-call | tf_op jit(solution)/shard_map/pallas_call | solution.py:383
  214.9 1.3 slice_reduce_fusion
  216.3 1.3 multiply_reduce_fusion
  217.6 2.2 copy.10
  219.7 8.4 %copy.11 = f32[32,128,512]{2,1,0:T(8,128)} copy(f32[32,128,512]{2,1,0:T(8,128)} %get-tuple-element.17) | data formatting | bytes 16777216

commit v3 on v2

--- a/solution.py
+++ b/solution.py
@@ -165,26 +165,26 @@
             device_id={"col": lax.rem(me + off, n)}, device_id_type=MESH,
         )
 
-    def mix(c_ref, b_ref):
+    def mix(it, c_ref, b_ref):
         for q in range(0, hl, 128):
             def add(k, total):
                 return total + c_ref[mine, pl.ds(k, 1), :] * b_ref[k, :, q : q + 128]
 
             mixed[:, q : q + 128] = jnp.tanh(lax.fori_loop(0, k_count, add, jnp.zeros((r, 128), F32)))
         for i, piece in enumerate(pieces(mixed[...])):
-            mixed_cut[i * r : (i + 1) * r, :] = piece
+            mixed_cut[it, i * r : (i + 1) * r, :] = piece
 
     step = rows // 4 if (rows // 4) % 16 == 0 else rows
 
-    def project():
-        cut = mixed_cut[...]
+    def project(it):
+        cut = mixed_cut[it]
         gram = fold_rows(fold(contract(cut, cut, ((1,), (1,))), r), r)
         for j in range(n):
             part[j, rows : rows + r, :] = gram
 
         def block(i, carry):
             at = pl.ds(pl.multiple_of(i * step, 16), step)
-            value = fold(contract(target[at, :], mixed_cut[...], ((1,), (1,))), r)
+            value = fold(contract(target[at, :], mixed_cut[it], ((1,), (1,))), r)
             j = i // (rows // step)
             part[j, pl.ds(pl.multiple_of((i - j * (rows // step)) * step, 8), step), :] = value
             return carry
@@ -221,25 +221,33 @@
         d_mixed = jnp.dot(gram, now, precision=HIGHEST, preferred_element_type=F32) - total[:, :hl]
         d_pre[it, mine] = d_mixed * scale * (1.0 - now * now)
 
-    def loss_of(it):
-        loss_sum[...] = jnp.zeros_like(loss_sum)
-
+    def loss_add(it, shard):
         def block(i, carry):
-            at = pl.ds(pl.multiple_of(i * 256, 256), 256)
+            at = pl.ds(pl.multiple_of(shard * rows + i * step, 16), step)
             one, two = pieces(full[it, at, :], 2)
             wide = jnp.concatenate([one, two, one, two], axis=1)
-            tall = jnp.concatenate(
-                [mixed_cut[:r], mixed_cut[:r], mixed_cut[r : 2 * r], mixed_cut[r : 2 * r]], axis=0
-            )
+            upper, lower = mixed_cut[it, :r], mixed_cut[it, r : 2 * r]
+            tall = jnp.concatenate([upper, upper, lower, lower], axis=0)
             residual = contract(wide, tall, ((1,), (0,))) - target[at, :].astype(F32)
-            loss_sum[...] += jnp.sum((residual * residual).reshape(32, 8, hl), axis=0)
+            loss_sum[...] += jnp.sum((residual * residual).reshape(step // 8, 8, hl), axis=0)
             return carry
 
-        lax.fori_loop(0, d // 256, block, 0)
+        lax.fori_loop(0, rows // step, block, 0)
+
+    def loss_step(it, t):
+        for way in range(2):
+            shard = me - t * (1 - 2 * way)
+
+            @pl.when((shard >= 0) & (shard < n))
+            def _():
+                loss_add(it, shard)
+
+    def loss_close(it):
         total = loss_sum[:, 0:128]
         for q in range(128, hl, 128):
             total = total + loss_sum[:, q : q + 128]
         loss_in[mine, it * 8 : it * 8 + 8, :] = total
+        loss_sum[...] = jnp.zeros_like(loss_sum)
 
     def combine(c_ref, it, k, q):
         total = c_ref[0, pl.ds(k, 1), :] * d_pre[it, 0, :, q : q + 128]
@@ -272,9 +280,9 @@
     loads[3].wait()
     expert_start(c_one, 0)
     loads[1].wait()
-    mix(c_one, bases)
+    mix(0, c_one, bases)
     loads[2].wait()
-    project()
+    project(0)
     scatter_step(0, 0)
     absorb_step(0, 0)
     for t in range(1, n):
@@ -297,7 +305,6 @@
 
     lax.fori_loop(0, rows // step, factor_one, 0)
     gather_step(1, 0)
-    loss_of(0)
     scatter_sent(0)
     gather_sent(0)
     expert_wait(d_pre.at[0], 1)
@@ -313,35 +320,48 @@
     d_coef[0, me, table : table + 8, :] = jnp.zeros((8, 128), F32)
     for off in range(1, n):
         coef_copy(0, off).start()
+    gather_step(1, 1)
     absorb_step(1, 0)
     for off in range(1, n):
         coef_copy(0, off).wait()
     c_two[...] = adam_first(c_one[...], coef_sum(0)[:table].reshape(experts, k_count, 128))
-    mix(c_two, b_out)
-    if n > 1:
-        gather_step(1, 1)
-    project()
+    mix(1, c_two, b_out)
+    project(1)
     scatter_step(1, 0)
     absorb_step(1, 1)
+    loss_sum[...] = jnp.zeros_like(loss_sum)
+
+    def loss_first(j, carry):
+        loss_add(0, j)
+        return carry
+
     for t in range(2, n):
         gather_step(1, t)
-        scatter_step(1, t - 1)
-        absorb_step(1, t)
+        if t < n - 1:
+            scatter_step(1, t - 1)
+            absorb_step(1, t)
+            if t == 2:
+                lax.fori_loop(0, n, loss_first, 0)
+                loss_close(0)
+                loss_add(1, me)
+                loss_step(1, 1)
+            loss_step(1, t)
+    absorb_step(1, n - 1)
     pre_gradient(1)
     expert_start(d_pre.at[1], 2)
-    loss_of(1)
+    scatter_step(1, n - 2)
+    loss_step(1, n - 1)
+    loss_close(1)
     expert_start(loss_in, 3)
     expert_wait(d_pre.at[1], 2)
     expert_wait(loss_in, 3)
 
-    def bases_two(k, carry):
+    def coefs_two(k, carry):
         for q in range(0, hl, 128):
-            values = b_out[k, :, q : q + 128]
-            coef_rows(1, k, q, values)
-            b_out[k, :, q : q + 128] = adam_second(values, combine(c_one, 0, k, q), combine(c_two, 1, k, q))
-        return carry
-
-    lax.fori_loop(0, k_count, bases_two, 0)
+            coef_rows(1, k, q, b_out[k, :, q : q + 128])
+        return carry
+
+    lax.fori_loop(0, k_count, coefs_two, 0)
     losses = loss_in[0]
     for e in range(1, experts):
         losses = losses + loss_in[e]
@@ -350,6 +370,14 @@
     d_coef[1, me, table + 2 : table + 8, :] = jnp.zeros((6, 128), F32)
     for off in range(1, n):
         coef_copy(1, off).start()
+
+    def bases_two(k, carry):
+        for q in range(0, hl, 128):
+            values = b_out[k, :, q : q + 128]
+            b_out[k, :, q : q + 128] = adam_second(values, combine(c_one, 0, k, q), combine(c_two, 1, k, q))
+        return carry
+
+    lax.fori_loop(0, k_count, bases_two, 0)
     scatter_step(1, n - 1)
 
     def factor_two(i, carry):
@@ -404,7 +432,7 @@
             pltpu.VMEM((rows, r), F32),
             pltpu.VMEM((3 * r, hl + 3 * r), F32),
             pltpu.VMEM((r, hl), F32),
-            pltpu.VMEM((3 * r, hl), BF16),
+            pltpu.VMEM((2, 3 * r, hl), BF16),
             pltpu.VMEM((8, hl), F32),
             dma((4,)),
             dma((2, 2, n - 1)),

time: 228 us -> 215 us (0.943)
  Pallas kernels: 213 us -> 200 us
    pallas_call x1, Pallas kernels: 213 us -> 200 us  [shards(): pl.pallas_call(functools.partial(kernel, n, experts), out_shape=(jax.Shap...]
where the time goes in v3:
time: 215 us
  Pallas kernels  200 us (93%)
  local copies, waits for them, and re-layouts  13.2 us (6%)
    pallas_call x1, Pallas kernels, shards(): pl.pallas_call(functools.partial(kernel, n, experts), out_shape=(jax.Shap...  200 us
    unnamed x2, local copies, waits for them, and re-layouts  10.5 us

profile of v3, /device:TPU:0, one launch (start us, length us, event | category | flops | bytes accessed | tf_op | source)
XLA Modules:
  0.0 215.1 jit_solution(11895293615971315922)
XLA Ops:
  0.6 1.3 broadcast_in_dim.11.c_in
  2.0 199.9 %shard_map.75 = (f32[1792,128]{1,0:T(8,128)}, f32[32,128,512]{2,1,0:T(8,128)}, f32[32,128]{1,0:T(8,128)}, f32[8,128]{1,0:T(8,128)}) custom-call(bf16[7168,512]{1,0:T(8,128)(2,1)} %bitcast.5, f32[1792,128]{1,0:T(8,128)} %bitcast.7, f32[32,128,512]{2,1,0:T(8,128)} %b_hbm.1, f32[32,128]{1,0:T(8,128)} %broadcast_in_dim.11.c_in), custom_call_target="tpu_custom_call" | custom-call | tf_op jit(solution)/shard_map/pallas_call | solution.py:411
  201.9 1.3 slice_reduce_fusion
  203.2 1.3 multiply_reduce_fusion
  204.5 2.2 %copy.10 = f32[1,1792,128]{2,1,0:T(8,128)} copy(f32[1,1792,128]{2,1,0:T(8,128)} %bitcast.6) | data formatting | bytes 1835008
  206.7 8.4 %copy.11 = f32[32,128,512]{2,1,0:T(8,128)} copy(f32[32,128,512]{2,1,0:T(8,128)} %get-tuple-element.17) | data formatting | bytes 16777216
